TPU v7x, 32 devices: a whole 2x2x4 slice. The times are simulated.
32 devices in a mesh: donor: 16 (over z, y, x), gene: 2 (over core).
Axes of the slice: x: 2, y: 2, z: 4, core: 2. Of those that a mesh axis runs over, the one named last changes fastest.
Arguments:
- embeddings: bfloat16 [32768, 512], P('donor', 'gene')
- targets_by_gene: bfloat16 [5120, 32768], P(('gene', 'donor')), may hold values from -6 to 6
- cell_counts: int32 [16], P('donor'), may hold values from 1024 to 2048, as said below
Outputs:
- coefficients: float32 [512, 5120], P('donor', 'gene')
Inputs may be any that keep to these rules, and one draw needn't show every extreme that they name: `cell_counts`: every entry is a multiple of 128; some entry equals 2048 and some entry equals 2048/2.
All inputs are finite; a program needn't handle non-finite values.
Results may differ from a plain program's by a relative error of at most 0.0003.
Values may be sent and summed in bfloat16 or wider, within the bound.
No kernel may reach another device: no remote copies, remote signals or barrier semaphores. Data moves between devices by JAX's collectives and lax.ppermute only.
A program may use at most 128 MiB of HBM per device.

v0:
```python
import math
import jax
import jax.numpy as jnp
from jax import lax
from jax.sharding import PartitionSpec as P


def solve_both(lower_factor, right_cols):
    halfway = lax.linalg.triangular_solve(lower_factor, right_cols, left_side=True, lower=True)
    return lax.linalg.triangular_solve(
        lower_factor, halfway, left_side=True, lower=True, transpose_a=True
    )


def shards(embeddings, targets_by_gene, cell_counts):
    valid_count = cell_counts[0]
    gathered = lax.all_gather(embeddings, "gene", axis=1, tiled=True)
    row_total = gathered.shape[0]
    width = gathered.shape[1]
    donors = lax.axis_size("donor")
    row_valid = lax.broadcasted_iota(jnp.int32, (row_total, 1), 0) < valid_count
    masked = jnp.where(row_valid, gathered, jnp.zeros_like(gathered))
    gram_matrix = lax.dot_general(
        masked, masked, (((0,), (0,)), ((), ())), preferred_element_type=jnp.float32
    )
    by_rows = lax.all_to_all(targets_by_gene, "donor", split_axis=1, concat_axis=0, tiled=True)
    gram_matrix = lax.psum(gram_matrix, "donor")
    lower_factor = jnp.linalg.cholesky(gram_matrix)
    scale_total = math.sqrt(row_total * donors)
    cross_local = jnp.dot(by_rows, masked, preferred_element_type=jnp.float32)
    cross_sum = lax.psum(cross_local, "donor")
    scaled = scale_total * solve_both(lower_factor, cross_sum.T)
    share = width // donors
    first_row = lax.axis_index("donor") * share
    return lax.dynamic_slice_in_dim(scaled, first_row, share, 0)


def solution(mesh):
    placed = (P("donor", "gene"), P(("gene", "donor"), None), P("donor"))
    return jax.shard_map(
        shards, mesh=mesh, in_specs=placed, out_specs=P("donor", "gene"), check_vma=False
    )
```

profile of v0, /device:TPU:0, one launch (start us, length us, event | category | flops | bytes accessed | tf_op | source)
XLA Modules:
  0.0 653.4 jit_solution(13016904788041452031)
XLA Ops:
  6.5 10.0 %copy.17 = bf16[20,16,8,2048]{3,2,0,1:T(8,128)(2,1)} copy(bf16[20,16,8,2048]{3,2,1,0:T(8,128)(2,1)} %bitcast.68) | data formatting | bytes 20971520 | tf_op jit(solution)/shard_map/all_to_all | solution.py:26
  16.6 8.4 %all-to-all-start = ((bf16[160,16,2048]{2,0,1:T(8,128)(2,1)}), bf16[160,16,2048]{2,0,1:T(8,128)(2,1)}, u32[]{:S(2)}, u32[]{:S(2)}) async-start(bf16[160,16,2048]{2,0,1:T(8,128)(2,1)} %bitcast.67), calls=%async_computation | async-start | bytes 20971520 | tf_op jit(solution)/shard_map/all_to_all | solution.py:26
  25.0 0.7 all-gather.2.cloned.1.call-update
  26.4 12.5 %all-gather.2.cloned.1.call-done = bf16[2048,512]{1,0:T(8,128)(2,1)} async-done(((bf16[2048,256]{1,0:T(8,128)(2,1)}), bf16[2048,512]{1,0:T(8,128)(2,1)}) %all-gather.2.cloned.1.call-update) | async-done | bytes 2097168 | tf_op jit(solution)/shard_map/all_gather | solution.py:17
  38.9 5.2 fusion.28
  44.1 178.5 %all-to-all-done = bf16[160,16,2048]{2,0,1:T(8,128)(2,1)} async-done(((bf16[160,16,2048]{2,0,1:T(8,128)(2,1)}), bf16[160,16,2048]{2,0,1:T(8,128)(2,1)}, u32[]{:S(2)}, u32[]{:S(2)}) %all-to-all-start) | async-done | bytes 10485792 | tf_op jit(solution)/shard_map/all_to_all | solution.py:26
  222.6 10.8 %fusion.27 = f32[512,2560]{1,0:T(8,128)} fusion(bf16[2560,2048]{1,0:T(8,128)(2,1)} %bitcast.10, bf16[2048,512]{1,0:T(8,128)(2,1)S(1)} %copy-done.1, pred[2048]{0:T(1024)(128)(4,1)S(1)} %iota_compare_fusion.3), kind=kOutput, calls=%fused_computation.43 | convolution fusion | flops 5369757696 | bytes 17827840 | tf_op jit(solution)/shard_map/dot_general | solution.py:30
  233.5 251.7 %all-reduce.4.cloned.1.call-done = (f32[512,2560]{1,0:T(8,128)}, f32[512,512]{0,1:T(8,128)}) async-done(((f32[512,2560]{1,0:T(8,128)}, f32[512,512]{0,1:T(8,128)}), (f32[512,2560]{1,0:T(8,128)}, f32[512,512]{0,1:T(8,128)})) %all-reduce.4.cloned.1.call-update) | async-done | bytes 6291472 | tf_op jit(solution)/shard_map/psum | solution.py:31
  485.2 1.6 copy.12
  487.1 11.7 %cholesky.104 = f32[128,128]{1,0:T(8,128)S(1)} custom-call(f32[128,128]{1,0:T(8,128)S(1)} %cholesky.266), custom_call_target="Cholesky" | custom-call | tf_op jit(solution)/shard_map/jit(cholesky)/cholesky | solution.py:28
  498.9 9.8 %custom-call.32 = f32[1,128,128]{1,2,0:T(8,128)S(1)} custom-call(f32[1,128,128]{2,1,0:T(8,128)S(1)} %get-tuple-element.34), custom_call_target="InvertDiagBlocksLowerTriangular" | custom-call | tf_op jit(solution)/shard_map/jit(cholesky)/cholesky | solution.py:28
  508.8 0.3 constant_dynamic-update-slice_fusion
  509.1 0.3 convolution_subtract_fusion.4
  509.4 11.7 %cholesky.217 = f32[128,128]{1,0:T(8,128)S(1)} custom-call(f32[128,128]{1,0:T(8,128)S(1)} %cholesky.270), custom_call_target="Cholesky" | custom-call | tf_op jit(solution)/shard_map/jit(cholesky)/cholesky | solution.py:28
  521.2 10.2 %custom-call.33 = f32[1,128,128]{1,2,0:T(8,128)S(1)} custom-call(f32[1,128,128]{2,1,0:T(8,128)S(1)} %get-tuple-element.31), custom_call_target="InvertDiagBlocksLowerTriangular" | custom-call | tf_op jit(solution)/shard_map/jit(cholesky)/cholesky | solution.py:28
  531.6 0.4 convolution_subtract_fusion.5
  532.0 11.7 %cholesky.238 = f32[128,128]{1,0:T(8,128)S(1)} custom-call(f32[128,128]{1,0:T(8,128)S(1)} %cholesky.275), custom_call_target="Cholesky" | custom-call | tf_op jit(solution)/shard_map/jit(cholesky)/cholesky | solution.py:28
  543.8 9.8 %custom-call.34 = f32[1,128,128]{1,2,0:T(8,128)S(1)} custom-call(f32[1,128,128]{2,1,0:T(8,128)S(1)} %get-tuple-element.28), custom_call_target="InvertDiagBlocksLowerTriangular" | custom-call | tf_op jit(solution)/shard_map/jit(cholesky)/cholesky | solution.py:28
  553.8 0.4 convolution_subtract_fusion.6
  554.2 11.7 %cholesky.255 = f32[128,128]{1,0:T(8,128)S(1)} custom-call(f32[128,128]{1,0:T(8,128)S(1)} %convolution_subtract_fusion.6), custom_call_target="Cholesky" | custom-call | tf_op jit(solution)/shard_map/jit(cholesky)/cholesky | solution.py:28
  566.0 0.7 compare_reduce_fusion.1
  566.6 0.7 compare_reduce_fusion
  567.3 0.7 compare_reduce_fusion.2
  570.9 10.6 %while.1 = (s32[]{:T(128)}, f32[512,512]{1,0:T(8,128)S(1)}, s32[4,2]{0,1:T(2,128)S(1)}, f32[4,128,128]{2,1,0:T(8,128)}, s32[]{:T(128)}) while((s32[]{:T(128)}, f32[512,512]{1,0:T(8,128)S(1)}, s32[4,2]{0,1:T(2,128)S(1)}, f32[4,128,128]{2,1,0:T(8,128)}, s32[]{:T(128)}) %tuple.27), condition=%wide.while_cond, body=%wide.while_body.sunk | while | flops 2 | bytes 132205 | solution.py:10
  571.0 0.6 fusion.76
  571.6 2.0 bitcast_dynamic-update-slice_fusion.2
  573.6 0.6 fusion.76
  574.2 2.0 bitcast_dynamic-update-slice_fusion.2
  576.3 0.6 fusion.76
  576.8 2.0 bitcast_dynamic-update-slice_fusion.2
  578.9 0.6 fusion.76
  579.5 2.0 bitcast_dynamic-update-slice_fusion.2
  581.5 40.1 %custom-call.35 = f32[4,128,128]{1,2,0:T(8,128)S(1)} custom-call(f32[4,128,128]{2,1,0:T(8,128)} %get-tuple-element.12), custom_call_target="InvertDiagBlocksLowerTriangular" | custom-call | tf_op jit(solution)/shard_map/triangular_solve | solution.py:10
  621.6 2.7 fusion.24
  624.3 2.6 convolution_subtract_fusion.1
  626.9 1.3 fusion.52
  628.2 1.5 convolution_subtract_fusion.3
  629.8 1.3 fusion.54
  631.0 2.5 fusion.15
  633.5 1.3 fusion.56
  634.8 1.3 fusion.55
  636.1 1.5 convolution_subtract_fusion
  637.6 1.3 fusion.53
  638.9 1.6 convolution_subtract_fusion.2
  640.4 1.3 fusion.51
  641.7 2.5 fusion.12
  644.2 1.3 fusion.50
  645.5 0.8 fusion.32
  (32 shorter events, 1.7 us)
Async XLA Ops:
  16.6 206.0 %all-to-all-start = ((bf16[160,16,2048]{2,0,1:T(8,128)(2,1)}), bf16[160,16,2048]{2,0,1:T(8,128)(2,1)}, u32[]{:S(2)}, u32[]{:S(2)}) async-start(bf16[160,16,2048]{2,0,1:T(8,128)(2,1)} %bitcast.67), calls=%async_computation | async-start | bytes 20971520 | tf_op jit(solution)/shard_map/all_to_all | solution.py:26
  24.9 14.0 %all-gather.2.cloned.1.call-start = ((), (), s32[]{:S(2)}) async-start(), calls=%async_computation.1 | async-start | bytes 3145728 | tf_op jit(solution)/shard_map/all_gather | solution.py:17
  25.7 459.5 %all-reduce.4.cloned.1.call-start = ((), (), s32[]{:S(2)}) async-start(), calls=%async_computation.2 | async-start | bytes 12582912 | tf_op jit(solution)/shard_map/psum | solution.py:31
  38.9 183.7 %copy-start.1 = (bf16[2048,512]{1,0:T(8,128)(2,1)S(1)}, bf16[2048,512]{1,0:T(8,128)(2,1)}, u32[]{:S(2)}) copy-start(bf16[2048,512]{1,0:T(8,128)(2,1)} %all-gather.2.cloned.1.call-done) | copy-start | bytes 6291460
  485.2 1.7 copy-start
  531.6 96.5 %slice-start = ((s8[5242880]{0:T(1024)(128)(4,1)}), s8[1048576]{0:T(1024)(128)(4,1)S(1)}, s32[]{:S(2)}) async-start(s8[5242880]{0:T(1024)(128)(4,1)} %bitcast.69), calls=%async_computation.3 | async-start | bytes 2097152
  621.6 6.6 %slice-start.1 = ((s8[5242880]{0:T(1024)(128)(4,1)}), s8[4194304]{0:T(1024)(128)(4,1)S(1)}, s32[]{:S(2)}) async-start(s8[5242880]{0:T(1024)(128)(4,1)} %bitcast.69), calls=%async_computation.4 | async-start | bytes 8388608
Sparse Core Ops, SparseCore 0:
  27.3 11.5 all-gather.1
  233.6 251.5 all-reduce.3
where the time goes:
time: 659 us; the launch traced here: 653 us
  waiting for transfers between devices  443 us (67%)
  other arithmetic  120 us (18%)
  matrix products  41.6 us (6%)
  local copies, waits for them, and re-layouts  22.4 us (3%)
  between operations  17.2 us (3%)
  starting transfers between devices  8.44 us (1%)
    psum x1, waiting for transfers between devices, shards(): cross_sum = lax.psum(cross_local, 'donor')  252 us
    all_to_all x1, waiting for transfers between devices, shards(): lax.all_to_all(targets_by_gene, 'donor', split_axis=1, concat_axis=0, til...  178 us
    another operation x14, other arithmetic, shards(): lower_factor = jnp.linalg.cholesky(gram_matrix)  78.9 us
    another operation x3, other arithmetic, solve_both(): lax.linalg.triangular_solve(lower_factor, halfway, left_side=True, lower=...  40.4 us
  transfers between devices with their start and end apart: 3, of which 3 were waited for; matrix products, arithmetic and copies ran while one was open for 1% of the time, Pallas kernels for 0%

commit v1 on v0

--- a/solution.py
+++ b/solution.py
@@ -1,8 +1,24 @@
+import functools
 import math
 import jax
 import jax.numpy as jnp
 from jax import lax
 from jax.sharding import PartitionSpec as P
+
+
+def turn_the_fields(s0, axis_tag):
+    return jnp.concatenate(
+        lax.all_to_all(
+            jnp.stack(jnp.split(s0, lax.axis_size(axis_tag), axis=1), axis=0),
+            axis_name=axis_tag,
+            split_axis=0,
+            concat_axis=0,
+        ),
+        axis=0,
+    )
+
+
+find_quarters = functools.partial(turn_the_fields, axis_tag="donor")
 
 
 def solve_both(lower_factor, right_cols):
@@ -23,7 +39,7 @@
     gram_matrix = lax.dot_general(
         masked, masked, (((0,), (0,)), ((), ())), preferred_element_type=jnp.float32
     )
-    by_rows = lax.all_to_all(targets_by_gene, "donor", split_axis=1, concat_axis=0, tiled=True)
+    by_rows = find_quarters(targets_by_gene)
     gram_matrix = lax.psum(gram_matrix, "donor")
     lower_factor = jnp.linalg.cholesky(gram_matrix)
     scale_total = math.sqrt(row_total * donors)

time: 659 us -> 681 us (1.033)
  local copies, waits for them, and re-layouts: 22.4 us -> 44.4 us
    unnamed x8 -> x23, local copies, waits for them, and re-layouts: 0.02 us -> 30 us
    all_to_all x1 -> x0, local copies, waits for them, and re-layouts: 10 us -> none  [shards(): lax.all_to_all(targets_by_gene, 'donor', split_axis=1, concat_axis=0, til...]
where the time goes in v1:
time: 681 us; the launch traced here: 675 us
  waiting for transfers between devices  443 us (65%)
  other arithmetic  120 us (18%)
  local copies, waits for them, and re-layouts  44.4 us (7%)
  matrix products  41.6 us (6%)
  between operations  17.2 us (3%)
  starting transfers between devices  8.44 us (1%)
    psum x1, waiting for transfers between devices, shards(): cross_sum = lax.psum(cross_local, 'donor')  252 us
    all_to_all x1, waiting for transfers between devices, turn_the_fields(): lax.all_to_all(jnp.stack(jnp.split(s0, lax.axis_size(axis_tag), axis=1),...  178 us
    another operation x14, other arithmetic, shards(): lower_factor = jnp.linalg.cholesky(gram_matrix)  78.9 us
    another operation x3, other arithmetic, solve_both(): lax.linalg.triangular_solve(lower_factor, halfway, left_side=True, lower=...  40.4 us
    unnamed x23, local copies, waits for them, and re-layouts  30 us
  transfers between devices with their start and end apart: 3, of which 3 were waited for; matrix products, arithmetic and copies ran while one was open for 1% of the time, Pallas kernels for 0%

profile of v1, /device:TPU:0, one launch (start us, length us, event | category | flops | bytes accessed | tf_op | source)
XLA Modules:
  0.0 675.4 jit_solution(8993087154338507687)
XLA Ops:
  6.5 2.0 bitcast_dynamic-update-slice_fusion.16
  8.5 2.0 bitcast_dynamic-update-slice_fusion.15
  10.5 2.0 bitcast_dynamic-update-slice_fusion.14
  12.5 2.0 bitcast_dynamic-update-slice_fusion.13
  14.5 2.0 bitcast_dynamic-update-slice_fusion.12
  16.5 2.0 bitcast_dynamic-update-slice_fusion.11
  18.5 2.0 bitcast_dynamic-update-slice_fusion.10
  20.5 2.0 bitcast_dynamic-update-slice_fusion.9
  22.5 2.0 bitcast_dynamic-update-slice_fusion.8
  24.5 2.0 bitcast_dynamic-update-slice_fusion.7
  26.5 2.0 bitcast_dynamic-update-slice_fusion.6
  28.5 2.0 bitcast_dynamic-update-slice_fusion.5
  30.5 2.0 bitcast_dynamic-update-slice_fusion.4
  32.5 2.0 bitcast_dynamic-update-slice_fusion.3
  34.5 2.0 bitcast_dynamic-update-slice_fusion.2
  36.5 2.0 bitcast_dynamic-update-slice_fusion.1
  38.5 8.4 %all-to-all-start = ((bf16[16,160,2048]{2,1,0:T(8,128)(2,1)}), bf16[16,160,2048]{2,1,0:T(8,128)(2,1)}, u32[]{:S(2)}, u32[]{:S(2)}) async-start(bf16[16,160,2048]{2,1,0:T(8,128)(2,1)} %bitcast_dynamic-update-slice_fusion.1), calls=%async_computation | async-start | bytes 20971520 | tf_op jit(solution)/shard_map/all_to_all | solution.py:11
  48.3 12.5 %all-gather.2.cloned.1.call-done = bf16[2048,512]{1,0:T(8,128)(2,1)} async-done(((bf16[2048,256]{1,0:T(8,128)(2,1)}), bf16[2048,512]{1,0:T(8,128)(2,1)}) %all-gather.2.cloned.1.call-update) | async-done | bytes 2097168 | tf_op jit(solution)/shard_map/all_gather | solution.py:33
  60.9 5.2 fusion.28
  66.1 178.5 %all-to-all-done = bf16[16,160,2048]{2,1,0:T(8,128)(2,1)} async-done(((bf16[16,160,2048]{2,1,0:T(8,128)(2,1)}), bf16[16,160,2048]{2,1,0:T(8,128)(2,1)}, u32[]{:S(2)}, u32[]{:S(2)}) %all-to-all-start) | async-done | bytes 10485792 | tf_op jit(solution)/shard_map/all_to_all | solution.py:11
  244.5 10.8 %fusion.27 = f32[512,2560]{1,0:T(8,128)} fusion(bf16[2560,2048]{1,0:T(8,128)(2,1)} %bitcast.25, bf16[2048,512]{1,0:T(8,128)(2,1)S(1)} %copy-done.1, pred[2048]{0:T(1024)(128)(4,1)S(1)} %iota_compare_fusion.3), kind=kOutput, calls=%fused_computation.42 | convolution fusion | flops 5369757696 | bytes 17827840 | tf_op jit(solution)/shard_map/dot_general | solution.py:46
  255.4 251.7 %all-reduce.4.cloned.1.call-done = (f32[512,2560]{1,0:T(8,128)}, f32[512,512]{0,1:T(8,128)}) async-done(((f32[512,2560]{1,0:T(8,128)}, f32[512,512]{0,1:T(8,128)}), (f32[512,2560]{1,0:T(8,128)}, f32[512,512]{0,1:T(8,128)})) %all-reduce.4.cloned.1.call-update) | async-done | bytes 6291472 | tf_op jit(solution)/shard_map/psum | solution.py:47
  507.1 1.6 copy.5
  509.0 11.7 %cholesky.104 = f32[128,128]{1,0:T(8,128)S(1)} custom-call(f32[128,128]{1,0:T(8,128)S(1)} %cholesky.266), custom_call_target="Cholesky" | custom-call | tf_op jit(solution)/shard_map/jit(cholesky)/cholesky | solution.py:44
  520.9 9.8 %custom-call.32 = f32[1,128,128]{1,2,0:T(8,128)S(1)} custom-call(f32[1,128,128]{2,1,0:T(8,128)S(1)} %get-tuple-element.34), custom_call_target="InvertDiagBlocksLowerTriangular" | custom-call | tf_op jit(solution)/shard_map/jit(cholesky)/cholesky | solution.py:44
  531.4 11.7 %cholesky.217 = f32[128,128]{1,0:T(8,128)S(1)} custom-call(f32[128,128]{1,0:T(8,128)S(1)} %cholesky.270), custom_call_target="Cholesky" | custom-call | tf_op jit(solution)/shard_map/jit(cholesky)/cholesky | solution.py:44
  543.2 10.2 %custom-call.33 = f32[1,128,128]{1,2,0:T(8,128)S(1)} custom-call(f32[1,128,128]{2,1,0:T(8,128)S(1)} %get-tuple-element.31), custom_call_target="InvertDiagBlocksLowerTriangular" | custom-call | tf_op jit(solution)/shard_map/jit(cholesky)/cholesky | solution.py:44
  554.0 11.7 %cholesky.238 = f32[128,128]{1,0:T(8,128)S(1)} custom-call(f32[128,128]{1,0:T(8,128)S(1)} %cholesky.275), custom_call_target="Cholesky" | custom-call | tf_op jit(solution)/shard_map/jit(cholesky)/cholesky | solution.py:44
  565.8 9.8 %custom-call.34 = f32[1,128,128]{1,2,0:T(8,128)S(1)} custom-call(f32[1,128,128]{2,1,0:T(8,128)S(1)} %get-tuple-element.28), custom_call_target="InvertDiagBlocksLowerTriangular" | custom-call | tf_op jit(solution)/shard_map/jit(cholesky)/cholesky | solution.py:44
  576.2 11.7 %cholesky.255 = f32[128,128]{1,0:T(8,128)S(1)} custom-call(f32[128,128]{1,0:T(8,128)S(1)} %convolution_subtract_fusion.6), custom_call_target="Cholesky" | custom-call | tf_op jit(solution)/shard_map/jit(cholesky)/cholesky | solution.py:44
  592.9 10.6 %while.1 = (s32[]{:T(128)}, f32[512,512]{1,0:T(8,128)S(1)}, s32[4,2]{0,1:T(2,128)S(1)}, f32[4,128,128]{2,1,0:T(8,128)}, s32[]{:T(128)}) while((s32[]{:T(128)}, f32[512,512]{1,0:T(8,128)S(1)}, s32[4,2]{0,1:T(2,128)S(1)}, f32[4,128,128]{2,1,0:T(8,128)}, s32[]{:T(128)}) %tuple.27), condition=%wide.while_cond, body=%wide.while_body.sunk | while | flops 2 | bytes 132205 | solution.py:26
  593.5 2.0 bitcast_dynamic-update-slice_fusion.18
  596.2 2.0 bitcast_dynamic-update-slice_fusion.18
  598.8 2.0 bitcast_dynamic-update-slice_fusion.18
  601.5 2.0 bitcast_dynamic-update-slice_fusion.18
  603.5 40.1 %custom-call.35 = f32[4,128,128]{1,2,0:T(8,128)S(1)} custom-call(f32[4,128,128]{2,1,0:T(8,128)} %get-tuple-element.12), custom_call_target="InvertDiagBlocksLowerTriangular" | custom-call | tf_op jit(solution)/shard_map/triangular_solve | solution.py:26
  643.6 2.7 fusion.24
  646.3 2.6 convolution_subtract_fusion.1
  648.9 1.3 fusion.52
  650.2 1.5 convolution_subtract_fusion.3
  651.7 1.3 fusion.54
  653.0 2.5 fusion.15
  655.5 1.3 fusion.56
  658.0 1.5 convolution_subtract_fusion
  660.8 1.6 convolution_subtract_fusion.2
  662.4 1.3 fusion.51
  663.7 2.5 fusion.12
  666.2 1.3 fusion.50
  (47 shorter events, 11.5 us)
Async XLA Ops:
  38.5 206.0 %all-to-all-start = ((bf16[16,160,2048]{2,1,0:T(8,128)(2,1)}), bf16[16,160,2048]{2,1,0:T(8,128)(2,1)}, u32[]{:S(2)}, u32[]{:S(2)}) async-start(bf16[16,160,2048]{2,1,0:T(8,128)(2,1)} %bitcast_dynamic-update-slice_fusion.1), calls=%async_computation | async-start | bytes 20971520 | tf_op jit(solution)/shard_map/all_to_all | solution.py:11
  46.9 14.0 %all-gather.2.cloned.1.call-start = ((), (), s32[]{:S(2)}) async-start(), calls=%async_computation.1 | async-start | bytes 3145728 | tf_op jit(solution)/shard_map/all_gather | solution.py:33
  47.6 459.5 %all-reduce.4.cloned.1.call-start = ((), (), s32[]{:S(2)}) async-start(), calls=%async_computation.2 | async-start | bytes 12582912 | tf_op jit(solution)/shard_map/psum | solution.py:47
  60.9 183.7 %copy-start.1 = (bf16[2048,512]{1,0:T(8,128)(2,1)S(1)}, bf16[2048,512]{1,0:T(8,128)(2,1)}, u32[]{:S(2)}) copy-start(bf16[2048,512]{1,0:T(8,128)(2,1)} %all-gather.2.cloned.1.call-done) | copy-start | bytes 6291460
  507.1 1.7 copy-start
  553.6 96.5 %slice-start = ((s8[5242880]{0:T(1024)(128)(4,1)}), s8[1048576]{0:T(1024)(128)(4,1)S(1)}, s32[]{:S(2)}) async-start(s8[5242880]{0:T(1024)(128)(4,1)} %bitcast.93), calls=%async_computation.3 | async-start | bytes 2097152
  643.6 6.6 slice-start.1
Sparse Core Ops, SparseCore 0:
  49.3 11.5 all-gather.1
  255.5 251.5 all-reduce.3
